TPU v7x, 32 devices: a whole 2x2x4 slice. The times are simulated.
32 devices in a mesh: fsdp: 4 (over y, core), ctx: 2 (over x), tp: 4 (over z).
Axes of the slice: x: 2, y: 2, z: 4, core: 2. Of those that a mesh axis runs over, the one named last changes fastest.
Arguments:
- tokens: bfloat16 [8, 1024, 1024], P('fsdp', 'ctx'), may hold values from -16 to 16
- gain1: bfloat16 [1024], P('fsdp'), may hold values from 0.5 to 1.5
- w_latent: bfloat16 [1024, 512], P('fsdp'), may hold values from -0.1875 to 0.1875
- w_query: bfloat16 [1024, 1024], P('fsdp', 'tp'), may hold values from -0.1875 to 0.1875
- w_key: bfloat16 [256, 1024], P('fsdp', 'tp'), may hold values from -0.375 to 0.375
- w_value: bfloat16 [256, 1024], P('fsdp', 'tp'), may hold values from -0.375 to 0.375
- w_out: bfloat16 [1024, 1024], P('tp', 'fsdp'), may hold values from -1.5 to 1.5
- gain2: bfloat16 [1024], P('fsdp'), may hold values from 0.5 to 1.5
- w_gate: bfloat16 [1024, 2816], P('fsdp', 'tp'), may hold values from -0.1875 to 0.1875
- w_up: bfloat16 [1024, 2816], P('fsdp', 'tp'), may hold values from -0.1875 to 0.1875
- w_down: bfloat16 [2816, 1024], P('tp', 'fsdp'), may hold values from -0.109375 to 0.109375
- segments: int32 [8, 1024], P('fsdp', 'ctx'), may hold values from 0 to 7, never falling along the last dimension, each value on 1 to 512 neighbouring positions
- cotangent: bfloat16 [8, 1024, 1024], P('fsdp', 'ctx'), may hold values from -6 to 6
Outputs:
- mixed: bfloat16 [8, 1024, 1024], P('fsdp', 'ctx')
- grad_tokens: bfloat16 [8, 1024, 1024], P('fsdp', 'ctx')
- grad_gain1: float32 [1024], P('fsdp')
- grad_latent: float32 [1024, 512], P('fsdp')
- grad_query: float32 [1024, 1024], P('fsdp', 'tp')
- grad_key: float32 [256, 1024], P('fsdp', 'tp')
- grad_value: float32 [256, 1024], P('fsdp', 'tp')
- grad_out: float32 [1024, 1024], P('tp', 'fsdp')
- grad_gain2: float32 [1024], P('fsdp')
- grad_gate: float32 [1024, 2816], P('fsdp', 'tp')
- grad_up: float32 [1024, 2816], P('fsdp', 'tp')
- grad_down: float32 [2816, 1024], P('tp', 'fsdp')
- stats: float32 [8, 3], P('fsdp')
- grad_radial: float32 [8, 1024], P('fsdp', 'ctx')
Inputs may be any that keep to these rules, and one draw needn't show every extreme that they name: `segments`: ids never fall along a sequence; every id of 0 to 7 names 1 to 512 consecutive tokens of each sequence, and some id names exactly 512; the largest id of a sequence marks its padding.
All inputs are finite; a program needn't handle non-finite values.
Results may differ from a plain program's by a relative error of at most 0.013.
The roundings to bfloat16 on the way count: a program that leaves them out, or rounds other values in their place, can miss the bound.
Values may be sent and summed in bfloat16 or wider, within the bound.
A program may use at most 128 MiB of HBM per device.

v0:
```python
import jax
import jax.numpy as jnp
from jax import lax
from jax.sharding import PartitionSpec as P

HEADS = 16
HEAD_DIM = 64
GROUPS = 2
LATENT = 256
eps = 1e-05


def precise(left, right):
    return jnp.dot(left, right, precision=lax.Precision.HIGHEST)


def block_scores(query_seq, key_seq, seg_keys, seg_query, q_place, block, tok_dev):
    key_blk = lax.dynamic_slice_in_dim(key_seq, block * tok_dev, tok_dev, 0)
    seg_blk = lax.dynamic_slice_in_dim(seg_keys, block * tok_dev, tok_dev, 0)
    k_place = block * tok_dev + jnp.arange(tok_dev, dtype=jnp.int32)
    counted = (k_place[None, :] <= q_place[:, None]) & (seg_blk[None, :] == seg_query[:, None])
    scores = (
        jnp.einsum("qhd,khd->hqk", query_seq, key_blk, preferred_element_type=jnp.float32) * 0.125
    )
    return (jnp.where(counted[None], scores, -1e30), counted, key_blk)


def norm_back(grad_norm, unit, scale, gain_f):
    scaled = grad_norm * gain_f
    return scale * (scaled - unit * jnp.mean(scaled * unit, axis=-1, keepdims=True))


def on_device(
    tokens,
    gain1,
    w_latent,
    w_query,
    w_key,
    w_value,
    w_out,
    gain2,
    w_gate,
    w_up,
    w_down,
    segments,
    cotangent,
):
    seq_dev, tok_dev, feat_dim = tokens.shape
    n_ctx = lax.axis_size("ctx")
    seq_len = tok_dev * n_ctx
    row_count = seq_dev * tok_dev
    gathered = (
        lax.all_gather(gain1, "fsdp", axis=0, tiled=True),
        lax.all_gather(w_latent, "fsdp", axis=0, tiled=True),
        lax.all_gather(w_query, "fsdp", axis=0, tiled=True),
        lax.all_gather(w_key, "fsdp", axis=0, tiled=True),
        lax.all_gather(w_value, "fsdp", axis=0, tiled=True),
        lax.all_gather(w_out, "fsdp", axis=1, tiled=True),
        lax.all_gather(gain2, "fsdp", axis=0, tiled=True),
        lax.all_gather(w_gate, "fsdp", axis=0, tiled=True),
        lax.all_gather(w_up, "fsdp", axis=0, tiled=True),
        lax.all_gather(w_down, "fsdp", axis=1, tiled=True),
    )
    g_one, w_lat, w_qry, w_kproj, w_vproj, w_outp, g_two, w_gatep, w_upp, w_downp = gathered
    heads_here = w_qry.shape[1] // HEAD_DIM
    q_width = heads_here * HEAD_DIM
    group_at = lax.axis_index("tp") * heads_here // (HEADS // GROUPS)
    lat_cols = lax.dynamic_slice_in_dim(w_lat, group_at * LATENT, LATENT, 1)
    stream = tokens.reshape(row_count, feat_dim).astype(jnp.float32)
    r_one = lax.rsqrt(jnp.mean(stream * stream, axis=-1, keepdims=True) + eps)
    unit_one = stream * r_one
    xn_one = (unit_one * g_one.astype(jnp.float32)).astype(jnp.bfloat16)
    latent = jnp.dot(xn_one, lat_cols, preferred_element_type=jnp.float32).astype(jnp.bfloat16)
    query = jnp.dot(xn_one, w_qry, preferred_element_type=jnp.float32).astype(jnp.bfloat16)
    query = query.reshape(seq_dev, tok_dev, heads_here, HEAD_DIM)
    lat_all, seg_all = (
        lax.all_gather(latent.reshape(seq_dev, tok_dev, LATENT), "ctx", axis=1, tiled=True),
        lax.all_gather(segments.astype(jnp.bfloat16), "ctx", axis=1, tiled=True),
    )
    keys = (
        jnp.dot(lat_all, w_kproj, preferred_element_type=jnp.float32)
        .astype(jnp.bfloat16)
        .reshape(seq_dev, seq_len, heads_here, HEAD_DIM)
    )
    values = (
        jnp.dot(lat_all, w_vproj, preferred_element_type=jnp.float32)
        .astype(jnp.bfloat16)
        .reshape(seq_dev, seq_len, heads_here, HEAD_DIM)
    )
    seg_keys = seg_all.astype(jnp.float32)
    seg_query = segments.astype(jnp.float32)
    ctx_at = lax.axis_index("ctx")
    q_place = ctx_at * tok_dev + jnp.arange(tok_dev, dtype=jnp.int32)
    last_blk = ctx_at + 1
    bounds = []
    lse_list = []
    attn_list = []
    for seq_at in range(seq_dev):
        query_seq = query[seq_at]
        key_seq = keys[seq_at]
        value_seq = values[seq_at]
        seg_k = seg_keys[seq_at]
        seg_q = seg_query[seq_at]
        block_last = seg_k.reshape(n_ctx, tok_dev)[:, -1]
        first_blk = jnp.sum((block_last < seg_q[0]).astype(jnp.int32))
        bounds.append(first_blk)

        def stat_step(block, carry, query_seq=query_seq, key_seq=key_seq, seg_k=seg_k, seg_q=seg_q):
            top, total = carry
            masked, counted, key_blk = block_scores(
                query_seq, key_seq, seg_k, seg_q, q_place, block, tok_dev
            )
            new_top = jnp.maximum(top, jnp.max(masked, axis=-1))
            total = total * jnp.exp(top - new_top) + jnp.sum(
                jnp.where(counted[None], jnp.exp(masked - new_top[..., None]), 0.0), axis=-1
            )
            return (new_top, total)

        start_stats = (
            jnp.full((heads_here, tok_dev), -1e30, jnp.float32),
            jnp.zeros((heads_here, tok_dev), jnp.float32),
        )
        top, total = lax.fori_loop(first_blk, last_blk, stat_step, start_stats)
        lse = top + jnp.log(total)
        lse_list.append(lse)

        def out_step(
            block,
            accum,
            query_seq=query_seq,
            key_seq=key_seq,
            value_seq=value_seq,
            seg_k=seg_k,
            seg_q=seg_q,
            lse=lse,
        ):
            masked, counted, key_blk = block_scores(
                query_seq, key_seq, seg_k, seg_q, q_place, block, tok_dev
            )
            value_blk = lax.dynamic_slice_in_dim(value_seq, block * tok_dev, tok_dev, 0)
            probs = jnp.where(counted[None], jnp.exp(masked - lse[..., None]), 0.0).astype(
                jnp.bfloat16
            )
            return accum + jnp.einsum(
                "hqk,khd->qhd", probs, value_blk, preferred_element_type=jnp.float32
            )

        accum = lax.fori_loop(
            first_blk, last_blk, out_step, jnp.zeros((tok_dev, heads_here, HEAD_DIM), jnp.float32)
        )
        attn_list.append(accum.astype(jnp.bfloat16).reshape(tok_dev, q_width))
    attended = jnp.concatenate(attn_list, axis=0)
    branch = lax.psum(jnp.dot(attended, w_outp, preferred_element_type=jnp.float32), "tp")
    middle = stream + branch
    r_two = lax.rsqrt(jnp.mean(middle * middle, axis=-1, keepdims=True) + eps)
    unit_two = middle * r_two
    xn_two = (unit_two * g_two.astype(jnp.float32)).astype(jnp.bfloat16)
    gate = jnp.dot(xn_two, w_gatep, preferred_element_type=jnp.float32)
    upper = jnp.dot(xn_two, w_upp, preferred_element_type=jnp.float32)
    sigma = jax.nn.sigmoid(gate)
    swish = gate * sigma
    hidden = (swish * upper).astype(jnp.bfloat16)
    feed = lax.psum(
        jnp.dot(hidden, w_downp, preferred_element_type=jnp.float32).astype(jnp.bfloat16), "tp"
    ).astype(jnp.float32)
    mixed = middle + feed
    valid = (seg_query != seg_keys[:, -1:]).astype(jnp.float32)
    valid_three = valid[:, :, None]

    def seq_squares(field):
        shaped = field.reshape(seq_dev, tok_dev, feat_dim)
        return jnp.sum(valid_three * shaped * shaped, axis=(1, 2))

    squares = jnp.stack([seq_squares(mixed), seq_squares(branch), seq_squares(feed)], axis=1)
    squares, counted_rows = lax.psum((squares, jnp.sum(valid, axis=1)), "ctx")
    stats = jnp.sqrt(squares / (counted_rows[:, None] * feat_dim))
    b_gone, b_lat, b_qry, b_kproj, b_vproj, b_outp, b_gtwo, b_gatep, b_upp, b_downp = gathered
    b_latcols = lax.dynamic_slice_in_dim(b_lat, group_at * LATENT, LATENT, 1)
    out_grad = cotangent.reshape(row_count, feat_dim)
    grad_down = jnp.dot(hidden.T, out_grad, preferred_element_type=jnp.float32)
    d_hidden = jnp.dot(out_grad, b_downp.T, preferred_element_type=jnp.float32)
    d_gate = (d_hidden * upper * sigma * (1.0 + gate * (1.0 - sigma))).astype(jnp.bfloat16)
    d_upper = (d_hidden * swish).astype(jnp.bfloat16)
    grad_gate = jnp.dot(xn_two.T, d_gate, preferred_element_type=jnp.float32)
    grad_up = jnp.dot(xn_two.T, d_upper, preferred_element_type=jnp.float32)
    part_two = jnp.dot(d_gate, b_gatep.T, preferred_element_type=jnp.float32) + jnp.dot(
        d_upper, b_upp.T, preferred_element_type=jnp.float32
    )
    d_xntwo = lax.psum(part_two, "tp")
    grad_gtwo = jnp.sum(d_xntwo * unit_two, axis=0)
    d_middle = out_grad.astype(jnp.float32) + norm_back(
        d_xntwo, unit_two, r_two, b_gtwo.astype(jnp.float32)
    )
    d_branch = d_middle.astype(jnp.bfloat16)
    grad_outp = jnp.dot(attended.T, d_branch, preferred_element_type=jnp.float32)
    d_attn = jnp.dot(d_branch, b_outp.T, preferred_element_type=jnp.float32).astype(jnp.bfloat16)
    d_attn = d_attn.reshape(seq_dev, tok_dev, heads_here, HEAD_DIM)
    dq_list = []
    dk_list = []
    dv_list = []
    for seq_at in range(seq_dev):
        query_seq = query[seq_at]
        key_seq = keys[seq_at]
        value_seq = values[seq_at]
        seg_k = seg_keys[seq_at]
        seg_q = seg_query[seq_at]
        lse = lse_list[seq_at]
        grad_seq = d_attn[seq_at]
        first_blk = bounds[seq_at]

        def delta_step(
            block,
            delta,
            query_seq=query_seq,
            key_seq=key_seq,
            value_seq=value_seq,
            seg_k=seg_k,
            seg_q=seg_q,
            lse=lse,
            grad_seq=grad_seq,
        ):
            masked, counted, key_blk = block_scores(
                query_seq, key_seq, seg_k, seg_q, q_place, block, tok_dev
            )
            value_blk = lax.dynamic_slice_in_dim(value_seq, block * tok_dev, tok_dev, 0)
            probs = jnp.where(counted[None], jnp.exp(masked - lse[..., None]), 0.0)
            d_prob = jnp.einsum(
                "qhd,khd->hqk", grad_seq, value_blk, preferred_element_type=jnp.float32
            )
            return delta + jnp.sum(probs * d_prob, axis=-1)

        delta = lax.fori_loop(
            first_blk, last_blk, delta_step, jnp.zeros((heads_here, tok_dev), jnp.float32)
        )

        def grad_step(
            block,
            carry,
            query_seq=query_seq,
            key_seq=key_seq,
            value_seq=value_seq,
            seg_k=seg_k,
            seg_q=seg_q,
            lse=lse,
            grad_seq=grad_seq,
            delta=delta,
        ):
            d_query, d_keys, d_values = carry
            masked, counted, key_blk = block_scores(
                query_seq, key_seq, seg_k, seg_q, q_place, block, tok_dev
            )
            value_blk = lax.dynamic_slice_in_dim(value_seq, block * tok_dev, tok_dev, 0)
            probs = jnp.where(counted[None], jnp.exp(masked - lse[..., None]), 0.0)
            d_prob = jnp.einsum(
                "qhd,khd->hqk", grad_seq, value_blk, preferred_element_type=jnp.float32
            )
            d_score = (probs * (d_prob - delta[..., None])).astype(jnp.bfloat16)
            d_query = d_query + 0.125 * jnp.einsum(
                "hqk,khd->qhd", d_score, key_blk, preferred_element_type=jnp.float32
            )
            d_keyblk = 0.125 * jnp.einsum(
                "hqk,qhd->khd", d_score, query_seq, preferred_element_type=jnp.float32
            )
            d_valblk = jnp.einsum(
                "hqk,qhd->khd",
                probs.astype(jnp.bfloat16),
                grad_seq,
                preferred_element_type=jnp.float32,
            )
            d_keys = lax.dynamic_update_slice_in_dim(d_keys, d_keyblk, block * tok_dev, 0)
            d_values = lax.dynamic_update_slice_in_dim(d_values, d_valblk, block * tok_dev, 0)
            return (d_query, d_keys, d_values)

        zero_keys = jnp.zeros((seq_len, heads_here, HEAD_DIM), jnp.float32)
        start_grads = (
            jnp.zeros((tok_dev, heads_here, HEAD_DIM), jnp.float32),
            zero_keys,
            zero_keys,
        )
        d_query, d_keys, d_values = lax.fori_loop(first_blk, last_blk, grad_step, start_grads)
        dq_list.append(d_query.astype(jnp.bfloat16).reshape(tok_dev, q_width))
        dk_list.append(d_keys.reshape(seq_len, q_width))
        dv_list.append(d_values.reshape(seq_len, q_width))
    d_query = jnp.concatenate(dq_list, axis=0)
    d_keys = jnp.stack(dk_list, axis=0)
    d_values = jnp.stack(dv_list, axis=0)
    own_keys, own_values = (
        lax.psum_scatter(d_keys, "ctx", scatter_dimension=1, tiled=True),
        lax.psum_scatter(d_values, "ctx", scatter_dimension=1, tiled=True),
    )
    own_keys = own_keys.reshape(row_count, q_width).astype(jnp.bfloat16)
    own_values = own_values.reshape(row_count, q_width).astype(jnp.bfloat16)
    grad_kproj = jnp.dot(latent.T, own_keys, preferred_element_type=jnp.float32)
    grad_vproj = jnp.dot(latent.T, own_values, preferred_element_type=jnp.float32)
    d_latent = jnp.dot(own_keys, b_kproj.T, preferred_element_type=jnp.float32) + jnp.dot(
        own_values, b_vproj.T, preferred_element_type=jnp.float32
    )
    grad_qry = jnp.dot(xn_one.T, d_query, preferred_element_type=jnp.float32)
    grad_latcols = precise(xn_one.astype(jnp.float32).T, d_latent)
    grad_lat = lax.dynamic_update_slice_in_dim(
        jnp.zeros((feat_dim, GROUPS * LATENT), jnp.float32), grad_latcols, group_at * LATENT, 1
    )
    part_one = jnp.dot(d_query, b_qry.T, preferred_element_type=jnp.float32) + precise(
        d_latent, b_latcols.astype(jnp.float32).T
    )
    d_xnone = lax.psum(part_one, "tp")
    grad_gone = jnp.sum(d_xnone * unit_one, axis=0)
    d_stream = d_middle + norm_back(d_xnone, unit_one, r_one, b_gone.astype(jnp.float32))
    radial = (jnp.sum(unit_one * d_stream, axis=-1) / jnp.sqrt(jnp.float32(feat_dim))).reshape(
        seq_dev, tok_dev
    )
    shards = (
        lax.psum_scatter(grad_gone, "fsdp", scatter_dimension=0, tiled=True),
        lax.psum_scatter(grad_lat, "fsdp", scatter_dimension=0, tiled=True),
        lax.psum_scatter(grad_qry, "fsdp", scatter_dimension=0, tiled=True),
        lax.psum_scatter(grad_kproj, "fsdp", scatter_dimension=0, tiled=True),
        lax.psum_scatter(grad_vproj, "fsdp", scatter_dimension=0, tiled=True),
        lax.psum_scatter(grad_outp, "fsdp", scatter_dimension=1, tiled=True),
        lax.psum_scatter(grad_gtwo, "fsdp", scatter_dimension=0, tiled=True),
        lax.psum_scatter(grad_gate, "fsdp", scatter_dimension=0, tiled=True),
        lax.psum_scatter(grad_up, "fsdp", scatter_dimension=0, tiled=True),
        lax.psum_scatter(grad_down, "fsdp", scatter_dimension=1, tiled=True),
    )
    s_gone, s_lat, s_qry, s_kproj, s_vproj, s_outp, s_gtwo, s_gate, s_upp, s_down = shards
    summed = lax.psum(
        (s_gone, s_qry, s_kproj, s_vproj, s_outp, s_gtwo, s_gate, s_upp, s_down), "ctx"
    )
    s_lat = lax.psum(s_lat, ("ctx", "tp"))
    f_gone, f_qry, f_kproj, f_vproj, f_outp, f_gtwo, f_gate, f_upp, f_down = summed
    mixed_out = mixed.reshape(seq_dev, tok_dev, feat_dim).astype(jnp.bfloat16)
    grad_tokens = d_stream.reshape(seq_dev, tok_dev, feat_dim).astype(jnp.bfloat16)
    return (
        mixed_out,
        grad_tokens,
        f_gone,
        s_lat,
        f_qry,
        f_kproj,
        f_vproj,
        f_outp,
        f_gtwo,
        f_gate,
        f_upp,
        f_down,
        stats,
        radial,
    )


def solution(mesh):
    return jax.shard_map(
        on_device,
        mesh=mesh,
        in_specs=(
            P("fsdp", "ctx", None),
            P("fsdp"),
            P("fsdp", None),
            P("fsdp", "tp"),
            P("fsdp", "tp"),
            P("fsdp", "tp"),
            P("tp", "fsdp"),
            P("fsdp"),
            P("fsdp", "tp"),
            P("fsdp", "tp"),
            P("tp", "fsdp"),
            P("fsdp", "ctx"),
            P("fsdp", "ctx", None),
        ),
        out_specs=(
            P("fsdp", "ctx", None),
            P("fsdp", "ctx", None),
            P("fsdp"),
            P("fsdp", None),
            P("fsdp", "tp"),
            P("fsdp", "tp"),
            P("fsdp", "tp"),
            P("tp", "fsdp"),
            P("fsdp"),
            P("fsdp", "tp"),
            P("fsdp", "tp"),
            P("tp", "fsdp"),
            P("fsdp", None),
            P("fsdp", "ctx"),
        ),
        check_vma=False,
    )
```

profile of v0, /device:TPU:0, one launch (start us, length us, event | category | flops | bytes accessed | tf_op | source)
XLA Modules:
  0.0 1288.4 jit_solution(14811559421376476977)
XLA Ops:
  10.8 6.0 all-gather
  25.2 7.9 all_gather.42
  33.1 7.5 all_gather.43
  45.9 5.4 all_gather.41
  60.2 7.7 all-gather.10.cloned.1.call-done
  92.5 158.9 %all-reduce.12.cloned.1.call-done = f32[1024,1024]{1,0:T(8,128)} async-done(((f32[1024,1024]{1,0:T(8,128)}), f32[1024,1024]{1,0:T(8,128)}) %all-reduce.12.cloned.1.call-update) | async-done | bytes 4194320 | tf_op jit(solution)/shard_map/psum | solution.py:153
  258.6 12.4 all-gather.12.cloned.1.call-done
  276.3 15.3 %all-gather.14.cloned.1.call-done = bf16[1024,704]{0,1:T(8,128)(2,1)} async-done(((bf16[256,704]{0,1:T(8,128)(2,1)}), bf16[1024,704]{0,1:T(8,128)(2,1)}) %all-gather.14.cloned.1.call-update) | async-done | bytes 1441808 | tf_op jit(solution)/shard_map/all_gather | solution.py:61
  296.9 15.3 %all-gather.16.cloned.1.call-done = bf16[704,1024]{1,0:T(8,128)(2,1)} async-done(((bf16[704,256]{1,0:T(8,128)(2,1)}), bf16[704,1024]{1,0:T(8,128)(2,1)}) %all-gather.16.cloned.1.call-update) | async-done | bytes 1441808 | tf_op jit(solution)/shard_map/all_gather | solution.py:62
  312.2 8.2 multiply_convert_fusion.1
  335.2 76.2 %all-reduce.14.cloned.1.call-done = bf16[1024,1024]{1,0:T(8,128)(2,1)} async-done(((bf16[1024,1024]{1,0:T(8,128)(2,1)}), bf16[1024,1024]{1,0:T(8,128)(2,1)}) %all-reduce.14.cloned.1.call-update) | async-done | bytes 2097168 | tf_op jit(solution)/shard_map/psum | solution.py:163
  411.4 156.3 %all-reduce.16.cloned.1.call-done = f32[1024,1024]{1,0:T(8,128)} async-done(((f32[1024,1024]{1,0:T(8,128)}), f32[1024,1024]{1,0:T(8,128)}) %all-reduce.16.cloned.1.call-update) | async-done | bytes 4194320 | tf_op jit(solution)/shard_map/psum | solution.py:189
  567.7 8.5 fusion.129
  586.1 9.7 while.105
  600.9 10.0 while.107
  643.4 25.1 %reduce-scatter.13.cloned.1.call-done = f32[2,512,256]{1,2,0:T(8,128)} async-done(((f32[2,1024,256]{1,2,0:T(8,128)}), f32[2,512,256]{1,2,0:T(8,128)}) %reduce-scatter.13.cloned.1.call-update) | async-done | bytes 1048592 | tf_op jit(solution)/shard_map/reduce_scatter | solution.py:289
  670.0 32.4 %reduce-scatter.11.cloned.1.call-done = f32[2,512,256]{1,2,0:T(8,128)} async-done(((f32[2,1024,256]{1,2,0:T(8,128)}), f32[2,512,256]{1,2,0:T(8,128)}) %reduce-scatter.11.cloned.1.call-update) | async-done | bytes 1048592 | tf_op jit(solution)/shard_map/reduce_scatter | solution.py:288
  707.9 6.2 convolution_add_fusion
  716.2 5.5 convolution_dynamic-update-slice_fusion
  721.7 19.8 %reduce-scatter.25.cloned.1.call-done = f32[256,704]{0,1:T(8,128)} async-done(((f32[1024,704]{0,1:T(8,128)}), f32[256,704]{0,1:T(8,128)}) %reduce-scatter.25.cloned.1.call-update) | async-done | bytes 720912 | tf_op jit(solution)/shard_map/reduce_scatter | solution.py:320
  741.6 38.8 %reduce-scatter.27.cloned.1.call-done = f32[256,704]{0,1:T(8,128)} async-done(((f32[1024,704]{0,1:T(8,128)}), f32[256,704]{0,1:T(8,128)}) %reduce-scatter.27.cloned.1.call-update) | async-done | bytes 720912 | tf_op jit(solution)/shard_map/reduce_scatter | solution.py:321
  780.3 39.1 %reduce-scatter.29.cloned.1.call-done = f32[704,256]{1,0:T(8,128)} async-done(((f32[704,1024]{1,0:T(8,128)}), f32[704,256]{1,0:T(8,128)}) %reduce-scatter.29.cloned.1.call-update) | async-done | bytes 720912 | tf_op jit(solution)/shard_map/reduce_scatter | solution.py:322
  819.4 27.3 %reduce-scatter.17.cloned.1.call-done = f32[256,256]{1,0:T(8,128)} async-done(((f32[1024,256]{1,0:T(8,128)}), f32[256,256]{1,0:T(8,128)}) %reduce-scatter.17.cloned.1.call-update) | async-done | bytes 262160 | tf_op jit(solution)/shard_map/reduce_scatter | solution.py:315
  846.7 27.4 %reduce-scatter.23.cloned.1.call-done = f32[256,256]{1,0:T(8,128)} async-done(((f32[256,1024]{1,0:T(8,128)}), f32[256,256]{1,0:T(8,128)}) %reduce-scatter.23.cloned.1.call-update) | async-done | bytes 262160 | tf_op jit(solution)/shard_map/reduce_scatter | solution.py:318
  874.2 23.0 %reduce-scatter.21.cloned.1.call-done = f32[64,256]{1,0:T(8,128)} async-done(((f32[256,256]{1,0:T(8,128)}), f32[64,256]{1,0:T(8,128)}) %reduce-scatter.21.cloned.1.call-update) | async-done | bytes 65552 | tf_op jit(solution)/shard_map/reduce_scatter | solution.py:317
  897.1 23.1 %reduce-scatter.19.cloned.1.call-done = f32[64,256]{1,0:T(8,128)} async-done(((f32[256,256]{1,0:T(8,128)}), f32[64,256]{1,0:T(8,128)}) %reduce-scatter.19.cloned.1.call-update) | async-done | bytes 65552 | tf_op jit(solution)/shard_map/reduce_scatter | solution.py:316
  922.2 155.3 %all-reduce.18.cloned.1.call-done = f32[1024,1024]{1,0:T(8,128)} async-done(((f32[1024,1024]{1,0:T(8,128)}), f32[1024,1024]{1,0:T(8,128)}) %all-reduce.18.cloned.1.call-update) | async-done | bytes 4194320 | tf_op jit(solution)/shard_map/psum | solution.py:306
  1085.7 7.0 all-reduce.2
  1092.9 5.5 all-reduce.3
  1098.4 12.2 reduce-scatter.15.cloned.1.call-done
  1112.0 81.0 %all-reduce.22.cloned.1.call-done = (f32[256,256]{1,0:T(8,128)}, f32[64,256]{1,0:T(8,128)}, f32[64,256]{1,0:T(8,128)}, f32[256,256]{1,0:T(8,128)}, f32[256,704]{...) async-done(((f32[256,256]{1,0:T(8,128)}, f32[64,256]{1,0:T(8,128)}, f32[64,256]{1,0:T(8,128)}, f32[256,256]{1,0:T(8,128)}, f32[256,704]{0,1:T(8,128)}, ...) | async-done | bytes 2818064 | tf_op jit(solution)/shard_map/psum | solution.py:325
  1193.0 76.2 %all-reduce.20.cloned.1.call-done = f32[256,512]{1,0:T(8,128)} async-done(((f32[256,512]{1,0:T(8,128)}), f32[256,512]{1,0:T(8,128)}) %all-reduce.20.cloned.1.call-update) | async-done | bytes 524304 | tf_op jit(solution)/shard_map/psum | solution.py:328
  (317 shorter events, 187.5 us)
Async XLA Ops:
  7.2 35.3 %all-gather.8.cloned.1.call-start = ((), (), s32[]{:S(2)}) async-start(), calls=%async_computation.10 | async-start | bytes 1310720 | tf_op jit(solution)/shard_map/all_gather | solution.py:54
  7.9 59.9 %all-gather.10.cloned.1.call-start = ((), (), s32[]{:S(2)}) async-start(), calls=%async_computation.11 | async-start | bytes 1572864 | tf_op jit(solution)/shard_map/all_gather | solution.py:77
  45.8 205.6 %all-reduce.12.cloned.1.call-start = ((), (), s32[]{:S(2)}) async-start(), calls=%async_computation.12 | async-start | bytes 8388608 | tf_op jit(solution)/shard_map/psum | solution.py:153
  85.6 185.4 %all-gather.12.cloned.1.call-start = ((), (), s32[]{:S(2)}) async-start(), calls=%async_computation.13 | async-start | bytes 1802240 | tf_op jit(solution)/shard_map/all_gather | solution.py:60
  86.2 205.4 %all-gather.14.cloned.1.call-start = ((), (), s32[]{:S(2)}) async-start(), calls=%async_computation.14 | async-start | bytes 1802240 | tf_op jit(solution)/shard_map/all_gather | solution.py:61
  86.8 225.4 %all-gather.16.cloned.1.call-start = ((), (), s32[]{:S(2)}) async-start(), calls=%async_computation.15 | async-start | bytes 1802240 | tf_op jit(solution)/shard_map/all_gather | solution.py:62
  87.4 324.0 %all-reduce.14.cloned.1.call-start = ((), (), s32[]{:S(2)}) async-start(), calls=%async_computation.16 | async-start | bytes 4194304 | tf_op jit(solution)/shard_map/psum | solution.py:163
  324.7 243.0 %all-reduce.16.cloned.1.call-start = ((), (), s32[]{:S(2)}) async-start(), calls=%async_computation.17 | async-start | bytes 8388608 | tf_op jit(solution)/shard_map/psum | solution.py:189
  332.9 335.6 %reduce-scatter.13.cloned.1.call-start = ((), (), s32[]{:S(2)}) async-start(), calls=%async_computation.19 | async-start | bytes 3145728 | tf_op jit(solution)/shard_map/reduce_scatter | solution.py:289
  335.1 241.1 %copy-start.45 = (f32[2]{0:T(128)}, f32[2]{0:T(128)S(1)}, u32[]{:S(2)}) copy-start(f32[2]{0:T(128)S(1)} %slice_reduce_fusion) | copy-start | bytes 28
  614.1 88.4 %reduce-scatter.11.cloned.1.call-start = ((), (), s32[]{:S(2)}) async-start(), calls=%async_computation.18 | async-start | bytes 3145728 | tf_op jit(solution)/shard_map/reduce_scatter | solution.py:288
  617.0 124.6 %reduce-scatter.25.cloned.1.call-start = ((), (), s32[]{:S(2)}) async-start(), calls=%async_computation.27 | async-start | bytes 3604480 | tf_op jit(solution)/shard_map/reduce_scatter | solution.py:320
  622.6 157.7 %reduce-scatter.27.cloned.1.call-start = ((), (), s32[]{:S(2)}) async-start(), calls=%async_computation.28 | async-start | bytes 3604480 | tf_op jit(solution)/shard_map/reduce_scatter | solution.py:321
  627.5 191.9 %reduce-scatter.29.cloned.1.call-start = ((), (), s32[]{:S(2)}) async-start(), calls=%async_computation.29 | async-start | bytes 3604480 | tf_op jit(solution)/shard_map/reduce_scatter | solution.py:322
  632.9 213.9 %reduce-scatter.17.cloned.1.call-start = ((), (), s32[]{:S(2)}) async-start(), calls=%async_computation.23 | async-start | bytes 1310720 | tf_op jit(solution)/shard_map/reduce_scatter | solution.py:315
  636.3 237.8 %reduce-scatter.23.cloned.1.call-start = ((), (), s32[]{:S(2)}) async-start(), calls=%async_computation.26 | async-start | bytes 1310720 | tf_op jit(solution)/shard_map/reduce_scatter | solution.py:318
  640.5 256.7 %reduce-scatter.21.cloned.1.call-start = ((), (), s32[]{:S(2)}) async-start(), calls=%async_computation.25 | async-start | bytes 327680 | tf_op jit(solution)/shard_map/reduce_scatter | solution.py:317
  705.1 215.2 %reduce-scatter.19.cloned.1.call-start = ((), (), s32[]{:S(2)}) async-start(), calls=%async_computation.24 | async-start | bytes 327680 | tf_op jit(solution)/shard_map/reduce_scatter | solution.py:316
  706.5 371.0 %all-reduce.18.cloned.1.call-start = ((), (), s32[]{:S(2)}) async-start(), calls=%async_computation.20 | async-start | bytes 8388608 | tf_op jit(solution)/shard_map/psum | solution.py:306
  714.2 396.5 %reduce-scatter.15.cloned.1.call-start = ((), (), s32[]{:S(2)}) async-start(), calls=%async_computation.21 | async-start | bytes 2621440 | tf_op jit(solution)/shard_map/reduce_scatter | solution.py:314
  716.1 204.2 %copy-start.50 = (u32[32]{0:T(128)S(1)}, u32[32]{0:T(128)}, u32[]{:S(2)}) copy-start(u32[32]{0:T(128)} %constant.179) | copy-start | bytes 388
  716.1 205.4 %copy-start.37 = (s32[2,512]{1,0:T(2,128)S(1)}, s32[2,512]{1,0:T(2,128)}, u32[]{:S(2)}) copy-start(s32[2,512]{1,0:T(2,128)} %param.40) | copy-start | bytes 12292
  716.1 205.4 %copy-start.46 = (f32[2]{0:T(128)S(1)}, f32[2]{0:T(128)}, u32[]{:S(2)}) copy-start(f32[2]{0:T(128)} %copy-done.45) | copy-start | bytes 28
  716.1 205.6 %copy-start.44 = (f32[1024]{0:T(1024)S(1)}, f32[1024]{0:T(1024)}, u32[]{:S(2)}) copy-start(f32[1024]{0:T(1024)} %get-tuple-element.1042) | copy-start | bytes 12292
  716.1 205.6 %copy-start.43 = (f32[1024]{0:T(1024)S(1)}, f32[1024]{0:T(1024)}, u32[]{:S(2)}) copy-start(f32[1024]{0:T(1024)} %get-tuple-element.823) | copy-start | bytes 12292
  716.1 205.7 %copy-start.42 = (f32[1024]{0:T(1024)S(1)}, f32[1024]{0:T(1024)}, u32[]{:S(2)}) copy-start(f32[1024]{0:T(1024)} %get-tuple-element.824) | copy-start | bytes 12292
  716.2 361.3 %copy-start.5 = (bf16[2,512,1024]{2,1,0:T(8,128)(2,1)S(1)}, bf16[2,512,1024]{2,1,0:T(8,128)(2,1)}, u32[]{:S(2)}) copy-start(bf16[2,512,1024]{2,1,0:T(8,128)(2,1)} %param.29) | copy-start | bytes 6291460
  716.2 361.3 %copy-start.33 = (f32[1,4,2,128]{3,1,2,0:T(4,128)S(1)}, f32[1,4,2,128]{3,1,2,0:T(4,128)}, u32[]{:S(2)}) copy-start(f32[1,4,2,128]{3,1,2,0:T(4,128)} %copy-done.32) | copy-start | bytes 12292
  716.2 361.3 %copy-start.35 = (f32[4,1,256]{2,1,0:T(1,128)S(1)}, f32[4,1,256]{2,1,0:T(1,128)}, u32[]{:S(2)}) copy-start(f32[4,1,256]{2,1,0:T(1,128)} %copy-done.34) | copy-start | bytes 12292
  721.7 471.3 %all-reduce.22.cloned.1.call-start = ((), (), s32[]{:S(2)}) async-start(), calls=%async_computation.30 | async-start | bytes 5636096 | tf_op jit(solution)/shard_map/psum | solution.py:325
  920.3 348.9 %all-reduce.20.cloned.1.call-start = ((), (), s32[]{:S(2)}) async-start(), calls=%async_computation.22 | async-start | bytes 1048576 | tf_op jit(solution)/shard_map/psum | solution.py:328
  1193.0 87.2 %copy-start.24 = (f32[704,256]{1,0:T(8,128)S(1)}, f32[704,256]{1,0:T(8,128)}, u32[]{:S(2)}) copy-start(f32[704,256]{1,0:T(8,128)} %get-tuple-element.2016) | copy-start | bytes 2162692
  (43 other events, 552.1 us)
Sparse Core Ops, SparseCore 0:
  9.6 19.4 all-gather.7
  45.9 21.8 all-gather.9
  85.7 165.5 all-reduce.11
  252.9 18.0 all-gather.11
  272.5 19.0 all-gather.13
  293.1 19.0 all-gather.15
  324.8 86.4 all-reduce.13
  413.7 153.9 all-reduce.15
  614.2 54.2 reduce-scatter.12
  670.6 31.8 reduce-scatter.10
  705.2 36.3 reduce-scatter.24
  744.0 36.3 reduce-scatter.26
  783.0 36.3 reduce-scatter.28
  821.8 24.8 reduce-scatter.16
  849.3 24.8 reduce-scatter.22
  877.1 20.0 reduce-scatter.20
  900.2 20.0 reduce-scatter.18
  922.4 154.9 all-reduce.17
  1080.2 30.4 reduce-scatter.14
  1113.2 79.7 all-reduce.21
  1196.8 72.3 all-reduce.19
where the time goes:
time: 1300 us; the launch traced here: 1290 us
  waiting for transfers between devices  1030 us (79%)
  matrix products  104 us (8%)
  blocking collectives  54.2 us (4%)
  other arithmetic  44.3 us (3%)
  local copies, waits for them, and re-layouts  32 us (2%)
  between operations  20.1 us (2%)
    psum x1, waiting for transfers between devices, on_device(): lax.psum(jnp.dot(attended, w_outp, preferred_element_type=jnp.float32), '...  159 us
    psum x1, waiting for transfers between devices, on_device(): d_xntwo = lax.psum(part_two, 'tp')  156 us
    psum x1, waiting for transfers between devices, on_device(): d_xnone = lax.psum(part_one, 'tp')  155 us
    psum x1, waiting for transfers between devices, on_device(): lax.psum((s_gone, s_qry, s_kproj, s_vproj, s_outp, s_gtwo, s_gate, s_upp,...  81 us
    psum x1, waiting for transfers between devices, on_device(): s_lat = lax.psum(s_lat, ('ctx', 'tp'))  76.2 us
    psum x1, waiting for transfers between devices, on_device(): lax.psum(jnp.dot(hidden, w_downp, preferred_element_type=jnp.float32).ast...  76.2 us
    reduce_scatter x1, waiting for transfers between devices, on_device(): lax.psum_scatter(grad_down, 'fsdp', scatter_dimension=1, tiled=True)  39.1 us
    reduce_scatter x1, waiting for transfers between devices, on_device(): lax.psum_scatter(grad_up, 'fsdp', scatter_dimension=0, tiled=True)  38.8 us
  transfers between devices with their start and end apart: 21, of which 20 were waited for; matrix products, arithmetic and copies ran while one was open for 7% of the time, Pallas kernels for 0%

commit v1 on v0

--- a/solution.py
+++ b/solution.py
@@ -325,7 +325,8 @@
     summed = lax.psum(
         (s_gone, s_qry, s_kproj, s_vproj, s_outp, s_gtwo, s_gate, s_upp, s_down), "ctx"
     )
-    s_lat = lax.psum(s_lat, ("ctx", "tp"))
+    for mesh_axis in ("tp", "ctx"):
+        s_lat = lax.psum(s_lat, mesh_axis)
     f_gone, f_qry, f_kproj, f_vproj, f_outp, f_gtwo, f_gate, f_upp, f_down = summed
     mixed_out = mixed.reshape(seq_dev, tok_dev, feat_dim).astype(jnp.bfloat16)
     grad_tokens = d_stream.reshape(seq_dev, tok_dev, feat_dim).astype(jnp.bfloat16)

time: 1300 us -> 1260 us (0.969)
  waiting for transfers between devices: 1030 us -> 988 us
    psum x2 -> x1, waiting for transfers between devices: 157 us -> 68.8 us  [on_device(): s_lat = lax.psum(s_lat, mesh_axis)]
    reduce_scatter x1, waiting for transfers between devices: 25.1 us -> 51.3 us  [on_device(): lax.psum_scatter(d_values, 'ctx', scatter_dimension=1, tiled=True)]
    psum x1, waiting for transfers between devices: 155 us -> 175 us  [on_device(): d_xnone = lax.psum(part_one, 'tp')]
    reduce_scatter x1, waiting for transfers between devices: 19.8 us -> 37.3 us  [on_device(): lax.psum_scatter(grad_gate, 'fsdp', scatter_dimension=0, tiled=True)]
  transfers between devices with their start and end apart: 21 -> 20, of which waited for: 20 -> 18; matrix products, arithmetic and copies ran while one was open for 7% -> 6% of each run, Pallas kernels for 0% -> 0%
where the time goes in v1:
time: 1260 us; the launch traced here: 1250 us
  waiting for transfers between devices  988 us (78%)
  matrix products  100 us (8%)
  blocking collectives  54.4 us (4%)
  other arithmetic  44.4 us (4%)
  local copies, waits for them, and re-layouts  32.7 us (3%)
  between operations  20.1 us (2%)
    psum x1, waiting for transfers between devices, on_device(): d_xnone = lax.psum(part_one, 'tp')  175 us
    psum x1, waiting for transfers between devices, on_device(): lax.psum(jnp.dot(attended, w_outp, preferred_element_type=jnp.float32), '...  159 us
    psum x1, waiting for transfers between devices, on_device(): d_xntwo = lax.psum(part_two, 'tp')  156 us
    psum x1, waiting for transfers between devices, on_device(): lax.psum(jnp.dot(hidden, w_downp, preferred_element_type=jnp.float32).ast...  76.2 us
    psum x1, waiting for transfers between devices, on_device(): s_lat = lax.psum(s_lat, mesh_axis)  68.8 us
    reduce_scatter x1, waiting for transfers between devices, on_device(): lax.psum_scatter(d_values, 'ctx', scatter_dimension=1, tiled=True)  51.3 us
    reduce_scatter x1, waiting for transfers between devices, on_device(): lax.psum_scatter(grad_up, 'fsdp', scatter_dimension=0, tiled=True)  39.1 us
    reduce_scatter x1, waiting for transfers between devices, on_device(): lax.psum_scatter(grad_down, 'fsdp', scatter_dimension=1, tiled=True)  38.8 us
  transfers between devices with their start and end apart: 20, of which 18 were waited for; matrix products, arithmetic and copies ran while one was open for 6% of the time, Pallas kernels for 0%

profile of v1, /device:TPU:0, one launch (start us, length us, event | category | flops | bytes accessed | tf_op | source)
XLA Modules:
  0.0 1248.3 jit_solution(5815373919866852711)
XLA Ops:
  10.8 6.0 all-gather
  25.2 7.9 all_gather.42
  33.1 7.5 all_gather.43
  45.9 5.4 all_gather.41
  53.9 5.4 all_gather.40
  60.2 7.7 all-gather.10.cloned.1.call-done
  92.6 158.8 %all-reduce.12.cloned.1.call-done = f32[1024,1024]{1,0:T(8,128)} async-done(((f32[1024,1024]{1,0:T(8,128)}), f32[1024,1024]{1,0:T(8,128)}) %all-reduce.12.cloned.1.call-update) | async-done | bytes 4194320 | tf_op jit(solution)/shard_map/psum | solution.py:153
  258.6 12.4 all-gather.12.cloned.1.call-done
  271.0 5.3 fusion.175
  276.3 15.3 %all-gather.14.cloned.1.call-done = bf16[1024,704]{0,1:T(8,128)(2,1)} async-done(((bf16[256,704]{0,1:T(8,128)(2,1)}), bf16[1024,704]{0,1:T(8,128)(2,1)}) %all-gather.14.cloned.1.call-update) | async-done | bytes 1441808 | tf_op jit(solution)/shard_map/all_gather | solution.py:61
  291.6 5.4 fusion.176
  297.0 15.3 %all-gather.16.cloned.1.call-done = bf16[704,1024]{1,0:T(8,128)(2,1)} async-done(((bf16[704,256]{1,0:T(8,128)(2,1)}), bf16[704,1024]{1,0:T(8,128)(2,1)}) %all-gather.16.cloned.1.call-update) | async-done | bytes 1441808 | tf_op jit(solution)/shard_map/all_gather | solution.py:62
  312.2 8.1 multiply_convert_fusion.1
  335.2 76.2 %all-reduce.14.cloned.1.call-done = bf16[1024,1024]{1,0:T(8,128)(2,1)} async-done(((bf16[1024,1024]{1,0:T(8,128)(2,1)}), bf16[1024,1024]{1,0:T(8,128)(2,1)}) %all-reduce.14.cloned.1.call-update) | async-done | bytes 2097168 | tf_op jit(solution)/shard_map/psum | solution.py:163
  411.4 156.3 %all-reduce.16.cloned.1.call-done = f32[1024,1024]{1,0:T(8,128)} async-done(((f32[1024,1024]{1,0:T(8,128)}), f32[1024,1024]{1,0:T(8,128)}) %all-reduce.16.cloned.1.call-update) | async-done | bytes 4194320 | tf_op jit(solution)/shard_map/psum | solution.py:189
  567.8 8.5 fusion.129
  586.1 9.7 while.105
  600.9 10.0 while.107
  617.3 51.3 %reduce-scatter.13.cloned.1.call-done = f32[2,512,256]{1,2,0:T(8,128)} async-done(((f32[2,1024,256]{1,2,0:T(8,128)}), f32[2,512,256]{1,2,0:T(8,128)}) %reduce-scatter.13.cloned.1.call-update) | async-done | bytes 1048592 | tf_op jit(solution)/shard_map/reduce_scatter | solution.py:289
  670.9 31.7 %reduce-scatter.11.cloned.1.call-done = f32[2,512,256]{1,2,0:T(8,128)} async-done(((f32[2,1024,256]{1,2,0:T(8,128)}), f32[2,512,256]{1,2,0:T(8,128)}) %reduce-scatter.11.cloned.1.call-update) | async-done | bytes 1048592 | tf_op jit(solution)/shard_map/reduce_scatter | solution.py:288
  716.7 5.3 fusion.183
  744.4 37.3 %reduce-scatter.25.cloned.1.call-done = f32[256,704]{0,1:T(8,128)} async-done(((f32[1024,704]{0,1:T(8,128)}), f32[256,704]{0,1:T(8,128)}) %reduce-scatter.25.cloned.1.call-update) | async-done | bytes 720912 | tf_op jit(solution)/shard_map/reduce_scatter | solution.py:320
  781.7 39.1 %reduce-scatter.27.cloned.1.call-done = f32[256,704]{0,1:T(8,128)} async-done(((f32[1024,704]{0,1:T(8,128)}), f32[256,704]{0,1:T(8,128)}) %reduce-scatter.27.cloned.1.call-update) | async-done | bytes 720912 | tf_op jit(solution)/shard_map/reduce_scatter | solution.py:321
  820.7 38.8 %reduce-scatter.29.cloned.1.call-done = f32[704,256]{1,0:T(8,128)} async-done(((f32[704,1024]{1,0:T(8,128)}), f32[704,256]{1,0:T(8,128)}) %reduce-scatter.29.cloned.1.call-update) | async-done | bytes 720912 | tf_op jit(solution)/shard_map/reduce_scatter | solution.py:322
  859.5 27.5 %reduce-scatter.17.cloned.1.call-done = f32[256,256]{1,0:T(8,128)} async-done(((f32[1024,256]{1,0:T(8,128)}), f32[256,256]{1,0:T(8,128)}) %reduce-scatter.17.cloned.1.call-update) | async-done | bytes 262160 | tf_op jit(solution)/shard_map/reduce_scatter | solution.py:315
  887.0 27.9 %reduce-scatter.23.cloned.1.call-done = f32[256,256]{1,0:T(8,128)} async-done(((f32[256,1024]{1,0:T(8,128)}), f32[256,256]{1,0:T(8,128)}) %reduce-scatter.23.cloned.1.call-update) | async-done | bytes 262160 | tf_op jit(solution)/shard_map/reduce_scatter | solution.py:318
  914.8 23.1 %reduce-scatter.21.cloned.1.call-done = f32[64,256]{1,0:T(8,128)} async-done(((f32[256,256]{1,0:T(8,128)}), f32[64,256]{1,0:T(8,128)}) %reduce-scatter.21.cloned.1.call-update) | async-done | bytes 65552 | tf_op jit(solution)/shard_map/reduce_scatter | solution.py:317
  938.0 23.0 %reduce-scatter.19.cloned.1.call-done = f32[64,256]{1,0:T(8,128)} async-done(((f32[256,256]{1,0:T(8,128)}), f32[64,256]{1,0:T(8,128)}) %reduce-scatter.19.cloned.1.call-update) | async-done | bytes 65552 | tf_op jit(solution)/shard_map/reduce_scatter | solution.py:316
  960.9 174.9 %all-reduce.18.cloned.1.call-done = (f32[1024,1024]{1,0:T(8,128)}, f32[256,512]{1,0:T(8,128)}) async-done(((f32[1024,1024]{1,0:T(8,128)}, f32[256,512]{1,0:T(8,128)}), (f32[1024,1024]{1,0:T(8,128)}, f32[256,512]{1,0:T(8,128)})) %all-reduce.18.cloned.1.call-update) | async-done | bytes 4718608 | tf_op jit(solution)/shard_map/psum | solution.py:306
  1146.0 7.1 all-reduce.3
  1153.3 5.7 all-reduce.4
  1160.2 68.8 %all-reduce.20.cloned.1.call-done = (f32[256,512]{1,0:T(8,128)}, f32[256,256]{1,0:T(8,128)}, f32[64,256]{1,0:T(8,128)}, f32[64,256]{1,0:T(8,128)}, f32[256,256]{...) async-done(((f32[256,512]{1,0:T(8,128)}, f32[256,256]{1,0:T(8,128)}, f32[64,256]{1,0:T(8,128)}, f32[64,256]{1,0:T(8,128)}, ...) | async-done | bytes 3342352 | tf_op jit(solution)/shard_map/psum | solution.py:329
  (326 shorter events, 175.1 us)
Async XLA Ops:
  7.2 35.3 %all-gather.8.cloned.1.call-start = ((), (), s32[]{:S(2)}) async-start(), calls=%async_computation.10 | async-start | bytes 1310720 | tf_op jit(solution)/shard_map/all_gather | solution.py:54
  7.9 60.0 %all-gather.10.cloned.1.call-start = ((), (), s32[]{:S(2)}) async-start(), calls=%async_computation.11 | async-start | bytes 1572864 | tf_op jit(solution)/shard_map/all_gather | solution.py:77
  45.8 205.6 %all-reduce.12.cloned.1.call-start = ((), (), s32[]{:S(2)}) async-start(), calls=%async_computation.12 | async-start | bytes 8388608 | tf_op jit(solution)/shard_map/psum | solution.py:153
  85.7 185.3 %all-gather.12.cloned.1.call-start = ((), (), s32[]{:S(2)}) async-start(), calls=%async_computation.13 | async-start | bytes 1802240 | tf_op jit(solution)/shard_map/all_gather | solution.py:60
  86.3 205.4 %all-gather.14.cloned.1.call-start = ((), (), s32[]{:S(2)}) async-start(), calls=%async_computation.14 | async-start | bytes 1802240 | tf_op jit(solution)/shard_map/all_gather | solution.py:61
  86.9 225.4 %all-gather.16.cloned.1.call-start = ((), (), s32[]{:S(2)}) async-start(), calls=%async_computation.15 | async-start | bytes 1802240 | tf_op jit(solution)/shard_map/all_gather | solution.py:62
  87.4 324.0 %all-reduce.14.cloned.1.call-start = ((), (), s32[]{:S(2)}) async-start(), calls=%async_computation.16 | async-start | bytes 4194304 | tf_op jit(solution)/shard_map/psum | solution.py:163
  324.8 243.0 %all-reduce.16.cloned.1.call-start = ((), (), s32[]{:S(2)}) async-start(), calls=%async_computation.17 | async-start | bytes 8388608 | tf_op jit(solution)/shard_map/psum | solution.py:189
  333.0 335.7 %reduce-scatter.13.cloned.1.call-start = ((), (), s32[]{:S(2)}) async-start(), calls=%async_computation.19 | async-start | bytes 3145728 | tf_op jit(solution)/shard_map/reduce_scatter | solution.py:289
  335.1 241.1 %copy-start.52 = (f32[2]{0:T(128)}, f32[2]{0:T(128)S(1)}, u32[]{:S(2)}) copy-start(f32[2]{0:T(128)S(1)} %slice_reduce_fusion) | copy-start | bytes 28
  614.2 88.4 %reduce-scatter.11.cloned.1.call-start = ((), (), s32[]{:S(2)}) async-start(), calls=%async_computation.18 | async-start | bytes 3145728 | tf_op jit(solution)/shard_map/reduce_scatter | solution.py:288
  617.0 87.1 %copy-start.23 = (bf16[256,256]{1,0:T(8,128)(2,1)S(1)}, bf16[256,256]{1,0:T(8,128)(2,1)}, u32[]{:S(2)}) copy-start(bf16[256,256]{1,0:T(8,128)(2,1)} %copy-done.22) | copy-start | bytes 393220
  617.0 87.4 %copy-start.25 = (bf16[256,256]{1,0:T(8,128)(2,1)S(1)}, bf16[256,256]{1,0:T(8,128)(2,1)}, u32[]{:S(2)}) copy-start(bf16[256,256]{1,0:T(8,128)(2,1)} %copy-done.24) | copy-start | bytes 393220
  617.0 127.3 %reduce-scatter.15.cloned.1.call-start = ((), (), s32[]{:S(2)}) async-start(), calls=%async_computation.20 | async-start | bytes 2621440 | tf_op jit(solution)/shard_map/reduce_scatter | solution.py:314
  711.3 70.4 %reduce-scatter.25.cloned.1.call-start = ((), (), s32[]{:S(2)}) async-start(), calls=%async_computation.25 | async-start | bytes 3604480 | tf_op jit(solution)/shard_map/reduce_scatter | solution.py:320
  716.6 104.1 %reduce-scatter.27.cloned.1.call-start = ((), (), s32[]{:S(2)}) async-start(), calls=%async_computation.26 | async-start | bytes 3604480 | tf_op jit(solution)/shard_map/reduce_scatter | solution.py:321
  722.0 137.5 %reduce-scatter.29.cloned.1.call-start = ((), (), s32[]{:S(2)}) async-start(), calls=%async_computation.27 | async-start | bytes 3604480 | tf_op jit(solution)/shard_map/reduce_scatter | solution.py:322
  727.4 159.6 %reduce-scatter.17.cloned.1.call-start = ((), (), s32[]{:S(2)}) async-start(), calls=%async_computation.21 | async-start | bytes 1310720 | tf_op jit(solution)/shard_map/reduce_scatter | solution.py:315
  731.7 183.1 %reduce-scatter.23.cloned.1.call-start = ((), (), s32[]{:S(2)}) async-start(), calls=%async_computation.24 | async-start | bytes 1310720 | tf_op jit(solution)/shard_map/reduce_scatter | solution.py:318
  735.8 202.2 %reduce-scatter.21.cloned.1.call-start = ((), (), s32[]{:S(2)}) async-start(), calls=%async_computation.23 | async-start | bytes 327680 | tf_op jit(solution)/shard_map/reduce_scatter | solution.py:317
  737.0 224.0 %reduce-scatter.19.cloned.1.call-start = ((), (), s32[]{:S(2)}) async-start(), calls=%async_computation.22 | async-start | bytes 327680 | tf_op jit(solution)/shard_map/reduce_scatter | solution.py:316
  738.1 397.8 %all-reduce.18.cloned.1.call-start = ((), (), s32[]{:S(2)}) async-start(), calls=%async_computation.28 | async-start | bytes 9437184 | tf_op jit(solution)/shard_map/psum | solution.py:306
  744.2 391.7 %copy-start.57 = (u32[32]{0:T(128)S(1)}, u32[32]{0:T(128)}, u32[]{:S(2)}) copy-start(u32[32]{0:T(128)} %constant.179) | copy-start | bytes 388
  744.2 392.9 %copy-start.44 = (s32[2,512]{1,0:T(2,128)S(1)}, s32[2,512]{1,0:T(2,128)}, u32[]{:S(2)}) copy-start(s32[2,512]{1,0:T(2,128)} %param.40) | copy-start | bytes 12292
  744.2 392.9 %copy-start.53 = (f32[2]{0:T(128)S(1)}, f32[2]{0:T(128)}, u32[]{:S(2)}) copy-start(f32[2]{0:T(128)} %copy-done.52) | copy-start | bytes 28
  744.2 393.1 %copy-start.51 = (f32[1024]{0:T(1024)S(1)}, f32[1024]{0:T(1024)}, u32[]{:S(2)}) copy-start(f32[1024]{0:T(1024)} %get-tuple-element.1045) | copy-start | bytes 12292
  744.2 393.1 %copy-start.50 = (f32[1024]{0:T(1024)S(1)}, f32[1024]{0:T(1024)}, u32[]{:S(2)}) copy-start(f32[1024]{0:T(1024)} %get-tuple-element.823) | copy-start | bytes 12292
  744.2 393.1 %copy-start.49 = (f32[1024]{0:T(1024)S(1)}, f32[1024]{0:T(1024)}, u32[]{:S(2)}) copy-start(f32[1024]{0:T(1024)} %get-tuple-element.824) | copy-start | bytes 12292
  744.2 393.5 %copy-start.5 = (bf16[2,512,1024]{2,1,0:T(8,128)(2,1)S(1)}, bf16[2,512,1024]{2,1,0:T(8,128)(2,1)}, u32[]{:S(2)}) copy-start(bf16[2,512,1024]{2,1,0:T(8,128)(2,1)} %param.29) | copy-start | bytes 6291460
  744.3 393.5 %copy-start.40 = (f32[1,4,2,128]{3,1,2,0:T(4,128)S(1)}, f32[1,4,2,128]{3,1,2,0:T(4,128)}, u32[]{:S(2)}) copy-start(f32[1,4,2,128]{3,1,2,0:T(4,128)} %copy-done.39) | copy-start | bytes 12292
  744.3 393.5 %copy-start.42 = (f32[4,1,256]{2,1,0:T(1,128)S(1)}, f32[4,1,256]{2,1,0:T(1,128)}, u32[]{:S(2)}) copy-start(f32[4,1,256]{2,1,0:T(1,128)} %copy-done.41) | copy-start | bytes 12292
  744.3 484.7 %all-reduce.20.cloned.1.call-start = ((), (), s32[]{:S(2)}) async-start(), calls=%async_computation.29 | async-start | bytes 6684672 | tf_op jit(solution)/shard_map/psum | solution.py:329
  (48 other events, 352.8 us)
Sparse Core Ops, SparseCore 0:
  9.6 19.4 all-gather.7
  46.0 21.8 all-gather.9
  85.8 165.5 all-reduce.11
  252.9 18.0 all-gather.11
  272.5 19.0 all-gather.13
  293.1 19.0 all-gather.15
  324.9 86.5 all-reduce.13
  413.8 153.9 all-reduce.15
  614.3 54.2 reduce-scatter.12
  670.7 31.8 reduce-scatter.10
  711.4 31.4 reduce-scatter.14
  745.3 36.3 reduce-scatter.24
  784.4 36.3 reduce-scatter.26
  823.1 36.3 reduce-scatter.28
  862.0 24.8 reduce-scatter.16
  889.9 24.8 reduce-scatter.22
  917.9 20.0 reduce-scatter.20
  940.9 20.0 reduce-scatter.18
  963.5 172.2 all-reduce.17
  1138.6 90.3 all-reduce.19
